TPU v7x, 32 devices: a whole 2x2x4 slice. The times are simulated.
32 devices in a mesh: groups: 2 (over y), space: 16 (over z, x, core).
Axes of the slice: x: 2, y: 2, z: 4, core: 2. Of those that a mesh axis runs over, the one named last changes fastest.
Arguments:
- modes: float32 [4, 128, 32, 64], P('groups', None, 'space'), parts along dimension 0, may hold values from -6 to 6
- cell_weight: float32 [32, 128], P('space', 'groups'), parts along dimension 1, may hold values from 0.5 to 2
- seeds: int32 [256], P(('groups', 'space')), parts along dimension 0, may hold values from 0 to 255
- coeff_table: float32 [256, 128], replicated, may hold values from -6 to 6
- force_table: float32 [256, 128], replicated, may hold values from -6 to 6
- visc_table: float32 [256], replicated, may hold values from 0.02 to 0.2
Outputs:
- coefficients: float32 [256, 128], P(('groups', 'space')), parts along dimension 0
There are 2 independent parts, one for each index of `groups`. A program takes and returns all parts, laid end to end along the dimension named above; an argument that names none is the same for every part. Nothing has to cross between parts.
All inputs are finite; a program needn't handle non-finite values.
Results may differ from a plain program's by a relative error of at most 0.00013.
Values sent between devices are 32-bit elements; how exact they have to be, the bound alone decides.
A program may use at most 64 MiB of HBM per device.

v0:
```python
import math
import jax
import jax.numpy as jnp
from jax import lax
from jax.sharding import PartitionSpec as P

STEPS = 2
TIME_STEP = 0.5


def padded_2(array, sides, width):
    for axis, dim in sides:
        devices, length = (lax.axis_size(axis), array.shape[dim])
        up = [(i, (i + 1) % devices) for i in range(devices)]
        down = [(j, i) for i, j in up]
        last = lax.slice_in_dim(array, length - width, length, axis=dim)
        first = lax.slice_in_dim(array, 0, width, axis=dim)
        before = lax.ppermute(last, axis, up)
        after = lax.ppermute(first, axis, down)
        array = jnp.concatenate([before, array, after], axis=dim)
    return array


def shards(modes, cell_weight, seeds, coeff_table, force_table, visc_table):
    mode_count = modes.shape[1]
    slab_cells = modes.shape[2]
    across = modes.shape[3]
    devices = lax.axis_size("space")
    cell_count = slab_cells * across
    total_cells = cell_count * devices
    padded = padded_2(modes, (("space", 2),), 2)
    slope_along = (
        padded[:, :, 0:slab_cells]
        - 8.0 * padded[:, :, 1 : slab_cells + 1]
        + 8.0 * padded[:, :, 3 : slab_cells + 3]
        - padded[:, :, 4 : slab_cells + 4]
    ) / 12.0
    slope_across = (
        jnp.roll(modes, 2, 3)
        - 8.0 * jnp.roll(modes, 1, 3)
        + 8.0 * jnp.roll(modes, -1, 3)
        - jnp.roll(modes, -2, 3)
    ) / 12.0
    slopes = jnp.stack([slope_along, slope_across]).reshape(2, 2, mode_count, cell_count)
    velocity = modes.reshape(2, mode_count, cell_count)
    cell_scale = cell_weight.reshape(cell_count) / total_cells
    weighted = velocity * cell_scale[None, None, :]
    diffusion = lax.psum(
        jnp.einsum(
            "taic,tajc->ij",
            slopes * cell_scale[None, None, None, :],
            slopes,
            precision=lax.Precision.HIGHEST,
        ),
        "space",
    )
    selector = (
        seeds[:, None] == jnp.arange(coeff_table.shape[0], dtype=jnp.int32)[None, :]
    ).astype(jnp.float32)
    coeffs = jnp.dot(selector, coeff_table, precision=lax.Precision.HIGHEST)
    forcing = jnp.dot(selector, force_table, precision=lax.Precision.HIGHEST)
    viscosity = jnp.dot(selector, visc_table, precision=lax.Precision.HIGHEST)
    own_count = coeffs.shape[0]

    def field_block(coeff_rows):
        flow = jnp.einsum("ni,aic->anc", coeff_rows, velocity, precision=lax.Precision.HIGHEST)
        grads = jnp.einsum("nk,takc->tanc", coeff_rows, slopes, precision=lax.Precision.HIGHEST)
        carried = jnp.sum(flow[:, None, :, :] * grads, axis=0)
        return jnp.einsum("aic,anc->ni", weighted, carried, precision=lax.Precision.HIGHEST)

    for repeat in range(STEPS):
        everyone = lax.all_gather(coeffs, "space", axis=0, tiled=True)
        rows_each = math.gcd(own_count * lax.axis_size("space"), 128)
        stacked = everyone.reshape(
            own_count * lax.axis_size("space") // rows_each, rows_each, mode_count
        )
        quadratic = lax.psum_scatter(
            lax.map(field_block, stacked).reshape(own_count * lax.axis_size("space"), mode_count),
            "space",
            scatter_dimension=0,
            tiled=True,
        )
        linear = jnp.dot(coeffs, diffusion, precision=lax.Precision.HIGHEST)
        coeffs = coeffs + TIME_STEP * (forcing - viscosity[:, None] * linear - quadratic)
    return coeffs


def solution(mesh):
    placed = (
        P("groups", None, "space", None),
        P("space", "groups"),
        P(("groups", "space")),
        P(),
        P(),
        P(),
    )
    return jax.shard_map(
        shards, mesh=mesh, in_specs=placed, out_specs=P(("groups", "space"), None), check_vma=False
    )
```

profile of v0, /device:TPU:8, one launch (start us, length us, event | category | flops | bytes accessed | tf_op | source)
XLA Modules:
  0.0 243.6 jit_solution(18027088971304564999)
XLA Ops:
  6.6 2.6 %collective-permute-start.1 = (f32[2,128,2,64]{1,3,2,0:T(8,128)}, f32[2,128,2,64]{1,3,2,0:T(8,128)S(1)}, u32[]{:S(2)}, u32[]{:S(2)}) collective-permute-start(f32[2,128,2,64]{1,3,2,0:T(8,128)} %param.6), channel_id=1, source_target_pairs={{1,0},{2,1},{3,2},{4,3},{5,4},{6,5},{7,6},{8,7},{9,8},{10,9},{11,1... | collective-permute-start | bytes 393224 | tf_op jit(solution)/shard_map/ppermute | solution.py:19
  9.2 1.0 slice_bitcast_fusion
  10.3 0.1 copy.35
  10.4 0.5 copy-done.4
  11.0 0.2 fusion.34
  11.2 18.1 %all_gather.6 = f32[128,128]{1,0:T(8,128)S(1)} all-gather(f32[8,128]{1,0:T(8,128)S(1)} %fusion.34), channel_id=1, replica_groups=mesh['groups'=2,'space'=16] {'space'}, dimensions={0}, use_global_device_ids=true | all-gather | bytes 69632 | tf_op jit(solution)/shard_map/all_gather | solution.py:72
  29.3 0.3 convolution_bitcast_fusion.3
  29.8 0.6 copy-done.5
  30.4 0.7 copy-done.7
  31.1 0.6 dynamic-slice.2
  32.3 0.2 fusion.33
  32.6 0.6 fusion.2
  33.2 1.0 convolution_bitcast_fusion.6
  34.3 1.0 convolution_bitcast_fusion.5
  35.4 0.6 copy-done.6
  36.0 0.2 convolution_bitcast_fusion.7
  36.2 90.3 %all-reduce.8.cloned.1.call-done = (f32[128,128]{1,0:T(8,128)}, f32[128,128]{1,0:T(8,128)}) async-done(((f32[128,128]{1,0:T(8,128)}, f32[128,128]{1,0:T(8,128)}), (f32[128,128]{1,0:T(8,128)}, f32[128,128]{1,0:T(8,128)})) %all-reduce.8.cloned.1.call-update) | async-done | bytes 131088 | tf_op jit(solution)/shard_map/psum | solution.py:48
  126.5 1.0 fusion.11
  127.4 16.9 %all_gather.7 = f32[128,128]{1,0:T(8,128)S(1)} all-gather(f32[8,128]{1,0:T(8,128)S(1)} %fusion.11), channel_id=1, replica_groups=mesh['groups'=2,'space'=16] {'space'}, dimensions={0}, use_global_device_ids=true | all-gather | bytes 69632 | tf_op jit(solution)/shard_map/all_gather | solution.py:72
  144.4 0.3 convolution_bitcast_fusion.2
  144.8 0.6 fusion.3
  145.4 1.0 convolution_bitcast_fusion.4
  146.4 88.9 %all-reduce.6.cloned.1.call-done = f32[128,128]{1,0:T(8,128)} async-done(((f32[128,128]{1,0:T(8,128)}), f32[128,128]{1,0:T(8,128)}) %all-reduce.6.cloned.1.call-update) | async-done | bytes 65552
  235.3 1.4 fusion.7
  (30 shorter events, 0.7 us)
Async XLA Ops:
  6.5 3.9 %copy-start = (f32[256,128]{1,0:T(8,128)S(1)}, f32[256,128]{1,0:T(8,128)}, u32[]{:S(2)}) copy-start(f32[256,128]{1,0:T(8,128)} %param.9) | copy-start | bytes 393220
  6.5 3.6 %copy-start.1 = (f32[2,128,2,64]{1,3,2,0:T(8,128)S(1)}, f32[2,128,2,64]{1,3,2,0:T(8,128)}, u32[]{:S(2)}) copy-start(f32[2,128,2,64]{1,3,2,0:T(8,128)} %param.6) | copy-start | bytes 393220
  6.5 119.9 %all-reduce.8.cloned.1.call-start = ((), (), s32[]{:S(2)}) async-start(), calls=%async_computation.1 | async-start | bytes 262144 | tf_op jit(solution)/shard_map/psum | solution.py:48
  6.5 26.0 %collective-permute-start = (f32[2,128,2,64]{1,3,2,0:T(8,128)}, f32[2,128,2,64]{1,3,2,0:T(8,128)S(1)}, u32[]{:S(2)}, u32[]{:S(2)}) collective-permute-start(f32[2,128,2,64]{1,3,2,0:T(8,128)} %param.6), channel_id=1, source_target_pairs={{0,1},{1,2},{2,3},{3,4},{4,5},{5,6},{6,7},{7,8},{8,9},{9,10},{10,1... | collective-permute-start | bytes 393224 | tf_op jit(solution)/shard_map/ppermute | solution.py:18
  6.6 25.9 %collective-permute-start.1 = (f32[2,128,2,64]{1,3,2,0:T(8,128)}, f32[2,128,2,64]{1,3,2,0:T(8,128)S(1)}, u32[]{:S(2)}, u32[]{:S(2)}) collective-permute-start(f32[2,128,2,64]{1,3,2,0:T(8,128)} %param.6), channel_id=1, source_target_pairs={{1,0},{2,1},{3,2},{4,3},{5,4},{6,5},{7,6},{8,7},{9,8},{10,9},{11,1... | collective-permute-start | bytes 393224 | tf_op jit(solution)/shard_map/ppermute | solution.py:19
  10.3 0.7 copy-start.4
  29.6 0.7 copy-start.5
  29.6 2.7 %copy-start.3 = (f32[256,128]{1,0:T(8,128)S(1)}, f32[256,128]{1,0:T(8,128)}, u32[]{:S(2)}) copy-start(f32[256,128]{1,0:T(8,128)} %param.10) | copy-start | bytes 393220
  30.4 0.7 copy-start.7
  35.3 0.7 copy-start.6
  35.3 200.0 %all-reduce.6.cloned.1.call-start = ((), (), s32[]{:S(2)}) async-start(), calls=%async_computation | async-start | bytes 131072
  146.4 88.9 %copy-start.2 = (f32[128,128]{1,0:T(8,128)S(1)}, f32[128,128]{1,0:T(8,128)}, u32[]{:S(2)}) copy-start(f32[128,128]{1,0:T(8,128)} %get-tuple-element.27) | copy-start | bytes 196612
Sparse Core Ops, SparseCore 0:
  35.4 90.9 all-reduce.7
  146.5 88.7 all-reduce.5
where the time goes:
time: 244 us
  waiting for transfers between devices  179 us (73%)
  blocking collectives  35 us (14%)
  between operations  14.2 us (6%)
  matrix products  7.78 us (3%)
  local copies, waits for them, and re-layouts  4.56 us (2%)
  starting transfers between devices  2.68 us (1%)
    psum x1, waiting for transfers between devices, shards(): lax.psum(jnp.einsum('taic,tajc->ij', slopes * cell_scale[None, None, None...  90.3 us
    unnamed x3, waiting for transfers between devices  88.9 us
    all_gather x2, blocking collectives, shards(): everyone = lax.all_gather(coeffs, 'space', axis=0, tiled=True)  35 us
  transfers between devices with their start and end apart: 4, of which 2 were waited for; matrix products, arithmetic and copies ran while one was open for 1% of the time, Pallas kernels for 0%

commit v1 on v0

--- a/solution.py
+++ b/solution.py
@@ -1,3 +1,4 @@
+import functools
 import math
 import jax
 import jax.numpy as jnp
@@ -6,6 +7,15 @@
 
 STEPS = 2
 TIME_STEP = 0.5
+
+
+def mark_the_node(inputs, peer_axis):
+    met_up = lax.all_gather(inputs, peer_axis)
+    all_values = jnp.sum(met_up, 0)
+    return all_values
+
+
+lay_series_all_by_axis = functools.partial(mark_the_node, peer_axis="space")
 
 
 def padded_2(array, sides, width):
@@ -45,14 +55,13 @@
     velocity = modes.reshape(2, mode_count, cell_count)
     cell_scale = cell_weight.reshape(cell_count) / total_cells
     weighted = velocity * cell_scale[None, None, :]
-    diffusion = lax.psum(
+    diffusion = lay_series_all_by_axis(
         jnp.einsum(
             "taic,tajc->ij",
             slopes * cell_scale[None, None, None, :],
             slopes,
             precision=lax.Precision.HIGHEST,
-        ),
-        "space",
+        )
     )
     selector = (
         seeds[:, None] == jnp.arange(coeff_table.shape[0], dtype=jnp.int32)[None, :]

time: 244 us -> 262 us (1.074)
  waiting for transfers between devices: 179 us -> 196 us
    unnamed x3 -> x5, waiting for transfers between devices: 88.9 us -> 180 us
    psum x1 -> x0, waiting for transfers between devices: 90.3 us -> none  [shards(): lax.psum(jnp.einsum('taic,tajc->ij', slopes * cell_scale[None, None, None...]
    all_gather x0 -> x1, waiting for transfers between devices: none -> 13.1 us  [mark_the_node(): met_up = lax.all_gather(inputs, peer_axis)]
    ppermute x1, waiting for transfers between devices: 0.01 us -> 2.65 us  [padded_2(): before = lax.ppermute(last, axis, up)]
  transfers between devices with their start and end apart: 4 -> 5, of which waited for: 2 -> 5; matrix products, arithmetic and copies ran while one was open for 1% -> 2% of each run, Pallas kernels for 0% -> 0%
where the time goes in v1:
time: 262 us
  waiting for transfers between devices  196 us (75%)
  blocking collectives  36.4 us (14%)
  between operations  13.9 us (5%)
  matrix products  7.58 us (3%)
  local copies, waits for them, and re-layouts  5.45 us (2%)
    unnamed x5, waiting for transfers between devices  180 us
    all_gather x2, blocking collectives, shards(): everyone = lax.all_gather(coeffs, 'space', axis=0, tiled=True)  36.4 us
    all_gather x1, waiting for transfers between devices, mark_the_node(): met_up = lax.all_gather(inputs, peer_axis)  13.1 us
  transfers between devices with their start and end apart: 5, of which 5 were waited for; matrix products, arithmetic and copies ran while one was open for 2% of the time, Pallas kernels for 0%

profile of v1, /device:TPU:8, one launch (start us, length us, event | category | flops | bytes accessed | tf_op | source)
XLA Modules:
  0.0 262.1 jit_solution(14714968671249141143)
XLA Ops:
  6.5 0.8 collective-permute-start.1
  7.4 1.0 slice_bitcast_fusion
  8.4 0.7 copy-done.4
  9.3 0.9 collective-permute-done.1
  10.2 2.7 %collective-permute-done = f32[2,128,2,64]{1,3,2,0:T(8,128)S(1)} collective-permute-done((f32[2,128,2,64]{1,3,2,0:T(8,128)}, f32[2,128,2,64]{1,3,2,0:T(8,128)S(1)}, u32[]{:S(2)}, u32[]{:S(2)}) %collective-permute-start) | collective-permute-done | bytes 131104 | tf_op jit(solution)/shard_map/ppermute | solution.py:28
  13.0 1.0 convolution_bitcast_fusion.6
  14.2 0.5 copy-done.3
  14.9 19.4 %all_gather.14 = f32[128,128]{1,0:T(8,128)S(1)} all-gather(f32[8,128]{1,0:T(8,128)S(1)} %fusion.34), channel_id=1, replica_groups=mesh['groups'=2,'space'=16] {'space'}, dimensions={0}, use_global_device_ids=true | all-gather | bytes 69632 | tf_op jit(solution)/shard_map/all_gather | solution.py:81
  34.4 0.3 convolution_bitcast_fusion.3
  34.8 0.8 copy-done.2
  35.7 0.6 fusion.2
  36.4 1.0 convolution_bitcast_fusion.5
  37.4 0.6 copy-done.5
  38.2 0.7 copy-done.6
  38.9 0.6 dynamic-slice.2
  40.1 13.1 %all-gather.3.cloned.1.call-done = f32[2048,128]{1,0:T(8,128)} async-done(((f32[128,128]{1,0:T(8,128)}), f32[2048,128]{1,0:T(8,128)}) %all-gather.3.cloned.1.call-update) | async-done | bytes 1048592 | tf_op jit(solution)/shard_map/all_gather | solution.py:13
  53.2 1.3 reduce_sum.29
  54.5 90.9 %all-reduce.5.cloned.1.call-done = f32[128,128]{1,0:T(8,128)} async-done(((f32[128,128]{1,0:T(8,128)}), f32[128,128]{1,0:T(8,128)}) %all-reduce.5.cloned.1.call-update) | async-done | bytes 65552
  145.5 0.8 fusion.11
  146.3 16.9 %all_gather.15 = f32[128,128]{1,0:T(8,128)S(1)} all-gather(f32[8,128]{1,0:T(8,128)S(1)} %fusion.11), channel_id=1, replica_groups=mesh['groups'=2,'space'=16] {'space'}, dimensions={0}, use_global_device_ids=true | all-gather | bytes 69632 | tf_op jit(solution)/shard_map/all_gather | solution.py:81
  163.6 0.6 fusion.3
  164.2 1.0 convolution_bitcast_fusion.4
  165.2 88.9 %all-reduce.7.cloned.1.call-done = f32[128,128]{1,0:T(8,128)} async-done(((f32[128,128]{1,0:T(8,128)}), f32[128,128]{1,0:T(8,128)}) %all-reduce.7.cloned.1.call-update) | async-done | bytes 65552
  254.1 1.5 fusion.7
  (32 shorter events, 1.7 us)
Async XLA Ops:
  6.5 7.7 %copy-start = (f32[256,128]{1,0:T(8,128)S(1)}, f32[256,128]{1,0:T(8,128)}, u32[]{:S(2)}) copy-start(f32[256,128]{1,0:T(8,128)} %param.9) | copy-start | bytes 393220
  6.5 1.8 copy-start.1
  6.5 46.7 %all-gather.3.cloned.1.call-start = ((), (), s32[]{:S(2)}) async-start(), calls=%async_computation | async-start | bytes 1114112 | tf_op jit(solution)/shard_map/all_gather | solution.py:13
  6.5 3.7 %collective-permute-start.1 = (f32[2,128,2,64]{1,3,2,0:T(8,128)}, f32[2,128,2,64]{1,3,2,0:T(8,128)S(1)}, u32[]{:S(2)}, u32[]{:S(2)}) collective-permute-start(f32[2,128,2,64]{1,3,2,0:T(8,128)} %param.6), channel_id=1, source_target_pairs={{1,0},{2,1},{3,2},{4,3},{5,4},{6,5},{7,6},{8,7},{9,8},{10,9},{11,1... | collective-permute-start | bytes 393224 | tf_op jit(solution)/shard_map/ppermute | solution.py:29
  7.4 5.5 %collective-permute-start = (f32[2,128,2,64]{1,3,2,0:T(8,128)}, f32[2,128,2,64]{1,3,2,0:T(8,128)S(1)}, u32[]{:S(2)}, u32[]{:S(2)}) collective-permute-start(f32[2,128,2,64]{1,3,2,0:T(8,128)} %param.6), channel_id=1, source_target_pairs={{0,1},{1,2},{2,3},{3,4},{4,5},{5,6},{6,7},{7,8},{8,9},{9,10},{10,1... | collective-permute-start | bytes 393224 | tf_op jit(solution)/shard_map/ppermute | solution.py:28
  8.4 0.7 copy-start.4
  14.0 131.4 %all-reduce.5.cloned.1.call-start = ((), (), s32[]{:S(2)}) async-start(), calls=%async_computation.1 | async-start | bytes 131072
  14.1 0.7 copy-start.3
  34.6 0.9 copy-start.2
  37.4 0.7 copy-start.5
  37.4 216.7 %all-reduce.7.cloned.1.call-start = ((), (), s32[]{:S(2)}) async-start(), calls=%async_computation.2 | async-start | bytes 131072
  38.2 0.7 copy-start.6
Sparse Core Ops, SparseCore 0:
  14.1 39.0 all-gather.2
  56.7 88.7 all-reduce.4
  165.4 88.6 all-reduce.6
